TPU v7x, 256 devices: a whole 4x4x8 slice. The times are simulated.
256 devices in a mesh: pairs: 32 (over x, z), tm: 8 (over y, core).
Axes of the slice: x: 4, y: 4, z: 8, core: 2. Of those that a mesh axis runs over, the one named last changes fastest.
Arguments:
- traces: float32 [16, 2048, 6144], P('tm', 'pairs'), may hold values from -64 to 64
- station_slot: int32 [2048], replicated, may hold values from 0 to 2047, as said below
- pair_stations: int32 [2048, 2], P('pairs'), may hold values from 0 to 2047, as said below
Outputs:
- correlation_stack: float32 [2048, 2048], P('tm', 'pairs')
Inputs may be any that keep to these rules, and one draw needn't show every extreme that they name: `station_slot`: A permutation: rows r * 64 to (r + 1) * 64 - 1 of traces are the stations of owner r. `pair_stations`: in each block of 64 pairs (the pairs of one device), at most 8 of the 128 pair ends name stations whose station_slot // 64 is one value, and in every block one value is named by exactly 8 ends. A pair may name one station twice.
All inputs are finite; a program needn't handle non-finite values.
Results may differ from a plain program's by a relative error of at most 0.011.
Values may be sent and summed in bfloat16 or wider, within the bound.
No kernel may reach another device: no remote copies, remote signals or barrier semaphores. Data moves between devices by JAX's collectives and lax.ppermute only.
A program may use at most 64 MiB of HBM per device.

v0:
```python
import math
import jax
import jax.numpy as jnp
from jax import lax
from jax.sharding import PartitionSpec as P

F = 1536
FLO = 32
LAG = 1024
two_pi = 6.283185307179586


def tapered_rows(traces):
    length = traces.shape[-1]
    sample_times = lax.iota(jnp.int32, length).astype(jnp.float32)
    hann_window = 0.5 - 0.5 * jnp.cos((sample_times + 0.5) * (two_pi / length))
    centred = traces - jnp.mean(traces, axis=-1, keepdims=True)
    return (centred * hann_window).astype(jnp.bfloat16)


def forward_table(first_row, row_count, length, first_bin, bins):
    sample_times = first_row + lax.iota(jnp.int32, row_count)
    frequencies = first_bin + lax.iota(jnp.int32, bins)
    phases = sample_times[:, None] * frequencies[None, :] % length
    angles = phases.astype(jnp.float32) * (two_pi / length)
    return jnp.concatenate([jnp.cos(angles), -jnp.sin(angles)], axis=1).astype(jnp.bfloat16)


def whiten(spectrum, bins):
    real_part = spectrum[..., :bins]
    imag_part = spectrum[..., bins:]
    energy = real_part * real_part + imag_part * imag_part
    water_level = jnp.mean(energy, axis=-1, keepdims=True)
    scaling = lax.rsqrt(energy + 0.1 * water_level + 1e-06)
    return jnp.concatenate([real_part * scaling, imag_part * scaling], axis=-1).astype(jnp.bfloat16)


def whiten_spectra(tapered, first_bin, bins):
    length = tapered.shape[1]
    block_rows = min(512, length)

    def add_block(step_index, running):
        first_row = step_index * block_rows
        segment = lax.dynamic_slice_in_dim(tapered, first_row, block_rows, 1)
        cos_table = forward_table(first_row, block_rows, length, first_bin, bins)
        return running + jnp.dot(segment, cos_table, preferred_element_type=jnp.float32)

    spectrum = lax.fori_loop(
        0, length // block_rows, add_block, jnp.zeros((tapered.shape[0], 2 * bins), jnp.float32)
    )
    return whiten(spectrum, bins)


def cross_spectra(left_ends, right_ends, bins):
    left_real = left_ends[..., :bins].astype(jnp.float32)
    left_imag = left_ends[..., bins:].astype(jnp.float32)
    right_real = right_ends[..., :bins].astype(jnp.float32)
    right_imag = right_ends[..., bins:].astype(jnp.float32)
    return jnp.concatenate(
        [
            left_real * right_real + left_imag * right_imag,
            left_imag * right_real - left_real * right_imag,
        ],
        axis=-1,
    )


def lag_block(stacked, first_row, row_count, first_bin, bins, length, half_span):
    lag_values = first_row + lax.iota(jnp.int32, row_count) - half_span
    frequencies = first_bin + lax.iota(jnp.int32, bins)
    phases = lag_values[:, None] * frequencies[None, :] % length
    angles = phases.astype(jnp.float32) * (two_pi / length)
    lag_table = jnp.concatenate([jnp.cos(angles), -jnp.sin(angles)], axis=1)
    return lax.dot_general(
        lag_table,
        stacked,
        (((1,), (1,)), ((), ())),
        precision=lax.Precision.HIGHEST,
        preferred_element_type=jnp.float32,
    )


def lag_rows(stacked, row_count, block_rows, length):

    def one_block(block_index):
        return lag_block(stacked, block_index * block_rows, block_rows, FLO, F, length, LAG)

    pieces = lax.map(one_block, jnp.arange(row_count // block_rows, dtype=jnp.int32))
    return pieces.reshape(row_count, stacked.shape[0])


def on_device(traces, station_slot, pair_stations):
    window_count, station_count, length = traces.shape
    pair_count = pair_stations.shape[0]
    blocks = lax.axis_size("pairs")
    capacity = 4 * pair_count // blocks
    own_index = lax.axis_index("pairs")
    every_pair = lax.all_gather(pair_stations, "pairs", axis=0, tiled=True)
    slot_ids = station_slot[every_pair.reshape(blocks, 2 * pair_count)]
    owners = slot_ids // station_count
    local_rows = slot_ids % station_count
    onehot = (owners[:, :, None] == lax.iota(jnp.int32, blocks)[None, None, :]).astype(jnp.int32)
    end_ranks = jnp.sum((jnp.cumsum(onehot, axis=1) - onehot) * onehot, axis=2)
    wanted = (owners == own_index)[:, :, None] & (
        end_ranks[:, :, None] == lax.iota(jnp.int32, capacity)[None, None, :]
    )
    send_rows = jnp.sum(jnp.where(wanted, local_rows[:, :, None], 0), axis=1)
    own_owners = lax.dynamic_index_in_dim(owners, own_index, 0, keepdims=False)
    own_ranks = lax.dynamic_index_in_dim(end_ranks, own_index, 0, keepdims=False)
    positions = own_owners * capacity + own_ranks
    tapered = tapered_rows(traces).reshape(window_count * station_count, length)
    spectra = whiten_spectra(tapered, FLO, F).reshape(window_count, station_count, 2 * F)
    received = lax.all_to_all(
        spectra[:, send_rows], "pairs", split_axis=1, concat_axis=1, tiled=True
    )
    held_windows = received.shape[0]
    flattened = received.reshape(held_windows, blocks * capacity, 2 * F)
    pair_ends = flattened[:, positions].reshape(held_windows, pair_count, 2, 2 * F)
    cross_terms = cross_spectra(pair_ends[:, :, 0], pair_ends[:, :, 1], F)
    stacked = jnp.sum(cross_terms, axis=0)
    lag_share = 2 * LAG // lax.axis_size("tm")
    normalizer = 1.0 / math.sqrt(F * window_count * lax.axis_size("tm"))
    block_rows = min(256, lag_share)
    return lax.psum_scatter(
        lag_rows(stacked, lax.axis_size("tm") * lag_share, block_rows, length) * normalizer,
        "tm",
        scatter_dimension=0,
        tiled=True,
    )


def solution(mesh):
    in_specs = (P("tm", "pairs", None), P(), P("pairs", None))
    out_specs = P("tm", "pairs")
    return jax.shard_map(
        on_device, mesh=mesh, in_specs=in_specs, out_specs=out_specs, check_vma=False
    )
```

profile of v0, /device:TPU:2, one launch (start us, length us, event | category | flops | bytes accessed | tf_op | source)
XLA Modules:
  0.0 505.4 jit_solution(11358334564074070772)
XLA Ops:
  11.0 200.6 %while.29 = (s32[]{:T(128)}, f32[128,3072]{1,0:T(8,128)}, bf16[128,6144]{1,0:T(8,128)(2,1)}, s32[]{:T(128)}, s32[]{:T(128)}, /*index=5*/s32[]{:T(128)}, s32[]{:T(128)}) while((s32[]{:T(128)}, f32[128,3072]{1,0:T(8,128)}, bf16[128,6144]{1,0:T(8,128)(2,1)}, s32[]{:T(128)}, s32[]{:T(128)}, /*index=5*/s32[]{:T(128)}, s32[]{:T(128)}) %tuple.80), condition=%wide.region_2.3_spmd.clone, body=%wide.region_1.2_spmd.clone.sunk | while | flops 419170304 | bytes 9584781 | solution.py:48
  11.0 13.5 %cosine_convert_fusion.2 = (bf16[512,1536]{1,0:T(8,128)(2,1)S(1)}, bf16[512,1536]{1,0:T(8,128)(2,1)S(1)}) fusion(s32[1536]{0:T(1024)S(1)} %iota_add_fusion.7, s32[512]{0:T(512)S(1)} %iota_add_fusion.8), kind=kLoop, calls=%fused_computation.29.clone.1 | loop fusion | flops 9437184 | bytes 3153920 | tf_op jit(solution)/shard_map/convert
  27.2 13.5 %cosine_convert_fusion.2 = (bf16[512,1536]{1,0:T(8,128)(2,1)S(1)}, bf16[512,1536]{1,0:T(8,128)(2,1)S(1)}) fusion(s32[1536]{0:T(1024)S(1)} %iota_add_fusion.7, s32[512]{0:T(512)S(1)} %iota_add_fusion.8), kind=kLoop, calls=%fused_computation.29.clone.1 | loop fusion | flops 9437184 | bytes 3153920 | tf_op jit(solution)/shard_map/convert
  40.8 3.2 convolution_add_fusion.2
  44.0 13.5 %cosine_convert_fusion.2 = (bf16[512,1536]{1,0:T(8,128)(2,1)S(1)}, bf16[512,1536]{1,0:T(8,128)(2,1)S(1)}) fusion(s32[1536]{0:T(1024)S(1)} %iota_add_fusion.7, s32[512]{0:T(512)S(1)} %iota_add_fusion.8), kind=kLoop, calls=%fused_computation.29.clone.1 | loop fusion | flops 9437184 | bytes 3153920 | tf_op jit(solution)/shard_map/convert
  57.5 3.2 convolution_add_fusion.2
  60.8 13.5 %cosine_convert_fusion.2 = (bf16[512,1536]{1,0:T(8,128)(2,1)S(1)}, bf16[512,1536]{1,0:T(8,128)(2,1)S(1)}) fusion(s32[1536]{0:T(1024)S(1)} %iota_add_fusion.7, s32[512]{0:T(512)S(1)} %iota_add_fusion.8), kind=kLoop, calls=%fused_computation.29.clone.1 | loop fusion | flops 9437184 | bytes 3153920 | tf_op jit(solution)/shard_map/convert
  74.3 3.2 convolution_add_fusion.2
  77.5 13.5 %cosine_convert_fusion.2 = (bf16[512,1536]{1,0:T(8,128)(2,1)S(1)}, bf16[512,1536]{1,0:T(8,128)(2,1)S(1)}) fusion(s32[1536]{0:T(1024)S(1)} %iota_add_fusion.7, s32[512]{0:T(512)S(1)} %iota_add_fusion.8), kind=kLoop, calls=%fused_computation.29.clone.1 | loop fusion | flops 9437184 | bytes 3153920 | tf_op jit(solution)/shard_map/convert
  91.1 3.2 convolution_add_fusion.2
  94.3 13.5 %cosine_convert_fusion.2 = (bf16[512,1536]{1,0:T(8,128)(2,1)S(1)}, bf16[512,1536]{1,0:T(8,128)(2,1)S(1)}) fusion(s32[1536]{0:T(1024)S(1)} %iota_add_fusion.7, s32[512]{0:T(512)S(1)} %iota_add_fusion.8), kind=kLoop, calls=%fused_computation.29.clone.1 | loop fusion | flops 9437184 | bytes 3153920 | tf_op jit(solution)/shard_map/convert
  107.8 3.2 convolution_add_fusion.2
  111.1 13.5 %cosine_convert_fusion.2 = (bf16[512,1536]{1,0:T(8,128)(2,1)S(1)}, bf16[512,1536]{1,0:T(8,128)(2,1)S(1)}) fusion(s32[1536]{0:T(1024)S(1)} %iota_add_fusion.7, s32[512]{0:T(512)S(1)} %iota_add_fusion.8), kind=kLoop, calls=%fused_computation.29.clone.1 | loop fusion | flops 9437184 | bytes 3153920 | tf_op jit(solution)/shard_map/convert
  124.6 3.2 convolution_add_fusion.2
  127.8 13.5 %cosine_convert_fusion.2 = (bf16[512,1536]{1,0:T(8,128)(2,1)S(1)}, bf16[512,1536]{1,0:T(8,128)(2,1)S(1)}) fusion(s32[1536]{0:T(1024)S(1)} %iota_add_fusion.7, s32[512]{0:T(512)S(1)} %iota_add_fusion.8), kind=kLoop, calls=%fused_computation.29.clone.1 | loop fusion | flops 9437184 | bytes 3153920 | tf_op jit(solution)/shard_map/convert
  141.4 3.2 convolution_add_fusion.2
  144.6 13.5 %cosine_convert_fusion.2 = (bf16[512,1536]{1,0:T(8,128)(2,1)S(1)}, bf16[512,1536]{1,0:T(8,128)(2,1)S(1)}) fusion(s32[1536]{0:T(1024)S(1)} %iota_add_fusion.7, s32[512]{0:T(512)S(1)} %iota_add_fusion.8), kind=kLoop, calls=%fused_computation.29.clone.1 | loop fusion | flops 9437184 | bytes 3153920 | tf_op jit(solution)/shard_map/convert
  158.1 3.2 convolution_add_fusion.2
  161.4 13.5 %cosine_convert_fusion.2 = (bf16[512,1536]{1,0:T(8,128)(2,1)S(1)}, bf16[512,1536]{1,0:T(8,128)(2,1)S(1)}) fusion(s32[1536]{0:T(1024)S(1)} %iota_add_fusion.7, s32[512]{0:T(512)S(1)} %iota_add_fusion.8), kind=kLoop, calls=%fused_computation.29.clone.1 | loop fusion | flops 9437184 | bytes 3153920 | tf_op jit(solution)/shard_map/convert
  174.9 3.2 convolution_add_fusion.2
  178.1 13.5 %cosine_convert_fusion.2 = (bf16[512,1536]{1,0:T(8,128)(2,1)S(1)}, bf16[512,1536]{1,0:T(8,128)(2,1)S(1)}) fusion(s32[1536]{0:T(1024)S(1)} %iota_add_fusion.7, s32[512]{0:T(512)S(1)} %iota_add_fusion.8), kind=kLoop, calls=%fused_computation.29.clone.1 | loop fusion | flops 9437184 | bytes 3153920 | tf_op jit(solution)/shard_map/convert
  191.7 3.2 convolution_add_fusion.2
  194.9 13.5 %cosine_convert_fusion.2 = (bf16[512,1536]{1,0:T(8,128)(2,1)S(1)}, bf16[512,1536]{1,0:T(8,128)(2,1)S(1)}) fusion(s32[1536]{0:T(1024)S(1)} %iota_add_fusion.7, s32[512]{0:T(512)S(1)} %iota_add_fusion.8), kind=kLoop, calls=%fused_computation.29.clone.1 | loop fusion | flops 9437184 | bytes 3153920 | tf_op jit(solution)/shard_map/convert
  208.4 3.2 convolution_add_fusion.2
  214.7 45.7 %all-gather = s32[32,64,2]{1,2,0:T(2,128)S(1)} all-gather(s32[1,64,2]{1,2,0:T(2,128)S(1)} %bitcast.77), channel_id=1, replica_groups=mesh['pairs'=32,'tm'=8] {'pairs'}, dimensions={0}, use_global_device_ids=true | all-gather | bytes 16896 | tf_op jit(solution)/shard_map/all_gather | solution.py:98
  260.6 23.0 %gather_fusion = s32[4096]{0:T(1024)S(1)} fusion(s32[2048]{0:T(1024)S(1)} %copy-done, s32[4096]{0:T(1024)S(1)} %bitcast_clamp_fusion), kind=kCustom, calls=%fused_computation | custom fusion | bytes 49152 | tf_op jit(solution)/shard_map/gather | solution.py:99
  283.7 3.3 fusion.31
  288.6 12.9 %gather_fusion.1 = bf16[256,2,3072]{2,1,0:T(2,128)(2,1)} fusion(bf16[2,64,3072]{2,0,1:T(2,128)(2,1)S(1)} %pad_maximum_fusion, s32[1024]{0:T(1024)S(1)} %pad_clamp_fusion.1), kind=kCustom, calls=%fused_computation.1 | custom fusion | bytes 6292480 | tf_op jit(solution)/shard_map/gather | solution.py:114
  301.4 6.9 %all-to-all-start = ((bf16[2,32,8,3072]{3,0,2,1:T(2,128)(2,1)}), bf16[2,32,8,3072]{3,0,2,1:T(2,128)(2,1)S(1)}, u32[]{:S(2)}, u32[]{:S(2)}) async-start(bf16[2,32,8,3072]{3,0,2,1:T(2,128)(2,1)} %bitcast.69), calls=%async_computation | async-start | bytes 6291456 | tf_op jit(solution)/shard_map/all_to_all | solution.py:113
  308.7 62.0 %all-to-all-done = bf16[2,32,8,3072]{3,0,2,1:T(2,128)(2,1)S(1)} async-done(((bf16[2,32,8,3072]{3,0,2,1:T(2,128)(2,1)}), bf16[2,32,8,3072]{3,0,2,1:T(2,128)(2,1)S(1)}, u32[]{:S(2)}, u32[]{:S(2)}) %all-to-all-start) | async-done | bytes 3145760 | tf_op jit(solution)/shard_map/all_to_all | solution.py:113
  370.6 4.8 gather_fusion.2
  379.5 86.6 %while.28 = (s32[]{:T(128)}, f32[8,256,64]{1,2,0:T(8,128)S(1)}, s32[8]{0:T(128)S(1)}, f32[64,3072]{1,0:T(8,128)S(1)}, s32[]{:T(128)}, /*index=5*/s32[1]{0:T(128)}) while((s32[]{:T(128)}, f32[8,256,64]{1,2,0:T(8,128)S(1)}, s32[8]{0:T(128)S(1)}, f32[64,3072]{1,0:T(8,128)S(1)}, s32[]{:T(128)}, /*index=5*/s32[1]{0:T(128)}) %tuple.81), condition=%wide.region_9.10_spmd, body=%wide.region_8.9_spmd.sunk | while | flops 608700416 | bytes 7157861 | solution.py:88
  380.9 6.4 %fusion.51 = (f32[256,1536]{1,0:T(8,128)S(1)}, f32[256,1536]{1,0:T(8,128)S(1)}) fusion(s32[1536]{0:T(1024)S(1)} %iota_add_fusion.6, s32[256]{0:T(256)S(1)} %add_add_fusion.2), kind=kLoop, calls=%fused_computation.14.clone.1 | loop fusion | flops 3932160 | bytes 3152896 | tf_op jit(solution)/shard_map/while/body/eval_jaxpr/cos | solution.py:73
  387.3 3.0 fusion.52
  391.7 6.4 %fusion.51 = (f32[256,1536]{1,0:T(8,128)S(1)}, f32[256,1536]{1,0:T(8,128)S(1)}) fusion(s32[1536]{0:T(1024)S(1)} %iota_add_fusion.6, s32[256]{0:T(256)S(1)} %add_add_fusion.2), kind=kLoop, calls=%fused_computation.14.clone.1 | loop fusion | flops 3932160 | bytes 3152896 | tf_op jit(solution)/shard_map/while/body/eval_jaxpr/cos | solution.py:73
  398.1 3.0 fusion.52
  402.5 6.4 %fusion.51 = (f32[256,1536]{1,0:T(8,128)S(1)}, f32[256,1536]{1,0:T(8,128)S(1)}) fusion(s32[1536]{0:T(1024)S(1)} %iota_add_fusion.6, s32[256]{0:T(256)S(1)} %add_add_fusion.2), kind=kLoop, calls=%fused_computation.14.clone.1 | loop fusion | flops 3932160 | bytes 3152896 | tf_op jit(solution)/shard_map/while/body/eval_jaxpr/cos | solution.py:73
  409.0 3.0 fusion.52
  413.4 6.4 %fusion.51 = (f32[256,1536]{1,0:T(8,128)S(1)}, f32[256,1536]{1,0:T(8,128)S(1)}) fusion(s32[1536]{0:T(1024)S(1)} %iota_add_fusion.6, s32[256]{0:T(256)S(1)} %add_add_fusion.2), kind=kLoop, calls=%fused_computation.14.clone.1 | loop fusion | flops 3932160 | bytes 3152896 | tf_op jit(solution)/shard_map/while/body/eval_jaxpr/cos | solution.py:73
  419.8 3.0 fusion.52
  424.2 6.4 %fusion.51 = (f32[256,1536]{1,0:T(8,128)S(1)}, f32[256,1536]{1,0:T(8,128)S(1)}) fusion(s32[1536]{0:T(1024)S(1)} %iota_add_fusion.6, s32[256]{0:T(256)S(1)} %add_add_fusion.2), kind=kLoop, calls=%fused_computation.14.clone.1 | loop fusion | flops 3932160 | bytes 3152896 | tf_op jit(solution)/shard_map/while/body/eval_jaxpr/cos | solution.py:73
  430.6 3.0 fusion.52
  435.0 6.4 %fusion.51 = (f32[256,1536]{1,0:T(8,128)S(1)}, f32[256,1536]{1,0:T(8,128)S(1)}) fusion(s32[1536]{0:T(1024)S(1)} %iota_add_fusion.6, s32[256]{0:T(256)S(1)} %add_add_fusion.2), kind=kLoop, calls=%fused_computation.14.clone.1 | loop fusion | flops 3932160 | bytes 3152896 | tf_op jit(solution)/shard_map/while/body/eval_jaxpr/cos | solution.py:73
  441.4 3.0 fusion.52
  445.8 6.4 %fusion.51 = (f32[256,1536]{1,0:T(8,128)S(1)}, f32[256,1536]{1,0:T(8,128)S(1)}) fusion(s32[1536]{0:T(1024)S(1)} %iota_add_fusion.6, s32[256]{0:T(256)S(1)} %add_add_fusion.2), kind=kLoop, calls=%fused_computation.14.clone.1 | loop fusion | flops 3932160 | bytes 3152896 | tf_op jit(solution)/shard_map/while/body/eval_jaxpr/cos | solution.py:73
  456.6 6.4 %fusion.51 = (f32[256,1536]{1,0:T(8,128)S(1)}, f32[256,1536]{1,0:T(8,128)S(1)}) fusion(s32[1536]{0:T(1024)S(1)} %iota_add_fusion.6, s32[256]{0:T(256)S(1)} %add_add_fusion.2), kind=kLoop, calls=%fused_computation.14.clone.1 | loop fusion | flops 3932160 | bytes 3152896 | tf_op jit(solution)/shard_map/while/body/eval_jaxpr/cos | solution.py:73
  463.1 3.0 fusion.52
  467.0 31.6 %reduce-scatter.2.cloned.1.call-done = f32[256,64]{0,1:T(8,128)} async-done(((f32[2048,64]{0,1:T(8,128)}), f32[256,64]{0,1:T(8,128)}) %reduce-scatter.2.cloned.1.call-update) | async-done | bytes 65552 | tf_op jit(solution)/shard_map/reduce_scatter | solution.py:124
  (95 shorter events, 25.6 us)
Async XLA Ops:
  6.5 254.0 %copy-start = (s32[2048]{0:T(1024)S(1)}, s32[2048]{0:T(1024)}, u32[]{:S(2)}) copy-start(s32[2048]{0:T(1024)} %param.8) | copy-start | bytes 24580
  6.7 2.8 copy-start.1
  211.7 1.9 copy-start.2
  213.5 1.1 copy-start.4
  301.4 69.2 %all-to-all-start = ((bf16[2,32,8,3072]{3,0,2,1:T(2,128)(2,1)}), bf16[2,32,8,3072]{3,0,2,1:T(2,128)(2,1)S(1)}, u32[]{:S(2)}, u32[]{:S(2)}) async-start(bf16[2,32,8,3072]{3,0,2,1:T(2,128)(2,1)} %bitcast.69), calls=%async_computation | async-start | bytes 6291456 | tf_op jit(solution)/shard_map/all_to_all | solution.py:113
  308.4 190.2 %reduce-scatter.2.cloned.1.call-start = ((), (), s32[]{:S(2)}) async-start(), calls=%async_computation.2 | async-start | bytes 589824 | tf_op jit(solution)/shard_map/reduce_scatter | solution.py:124
  378.5 1.0 copy-start.3
Sparse Core Ops, SparseCore 0:
  467.1 31.3 reduce-scatter.1
where the time goes:
time: 506 us; the launch traced here: 505 us
  other arithmetic  225 us (44%)
  waiting for transfers between devices  93.5 us (18%)
  matrix products  62.1 us (12%)
  local copies, waits for them, and re-layouts  52.5 us (10%)
  blocking collectives  45.7 us (9%)
  between operations  13.6 us (3%)
  starting transfers between devices  7.16 us (1%)
  loops' own time  5.98 us (1%)
    another operation x13, other arithmetic  163 us
    all_to_all x1, waiting for transfers between devices, on_device(): lax.all_to_all(spectra[:, send_rows], 'pairs', split_axis=1, concat_axis=...  62 us
    cos x8, other arithmetic, lag_block(): lag_table = jnp.concatenate([jnp.cos(angles), -jnp.sin(angles)], axis=1)  51.4 us
    all_gather x1, blocking collectives, on_device(): every_pair = lax.all_gather(pair_stations, 'pairs', axis=0, tiled=True)  45.7 us
    dot_general x12, matrix products, add_block(): jnp.dot(segment, cos_table, preferred_element_type=jnp.float32)  38.1 us
    reduce_scatter x1, waiting for transfers between devices, on_device(): lax.psum_scatter(lag_rows(stacked, lax.axis_size('tm') * lag_share, block...  31.6 us
    dot_general x8, matrix products, lag_block(): lax.dot_general(lag_table, stacked, (((1,), (1,)), ((), ())), precision=l...  23.9 us
    gather x1, local copies, waits for them, and re-layouts, on_device(): slot_ids = station_slot[every_pair.reshape(blocks, 2 * pair_count)]  23 us
  transfers between devices with their start and end apart: 2, of which 2 were waited for; matrix products, arithmetic and copies ran while one was open for 0% of the time, Pallas kernels for 0%

commit v1 on v0

--- a/solution.py
+++ b/solution.py
@@ -95,7 +95,10 @@
     blocks = lax.axis_size("pairs")
     capacity = 4 * pair_count // blocks
     own_index = lax.axis_index("pairs")
-    every_pair = lax.all_gather(pair_stations, "pairs", axis=0, tiled=True)
+    n_dev = lax.axis_size("pairs")
+    parts = jnp.stack([pair_stations for _ in range(n_dev)])
+    parts = lax.all_to_all(parts, "pairs", split_axis=0, concat_axis=0)
+    every_pair = jnp.concatenate(parts, axis=0)
     slot_ids = station_slot[every_pair.reshape(blocks, 2 * pair_count)]
     owners = slot_ids // station_count
     local_rows = slot_ids % station_count

time: 506 us -> 487 us (0.962)
  blocking collectives: 45.7 us -> 0 us
  starting transfers between devices: 7.16 us -> 21.4 us
  waiting for transfers between devices: 93.5 us -> 104 us
    all_gather x1 -> x0, blocking collectives: 45.7 us -> none  [on_device(): every_pair = lax.all_gather(pair_stations, 'pairs', axis=0, tiled=True)]
    all_to_all x0 -> x1, starting transfers between devices: none -> 11.6 us  [on_device(): parts = lax.all_to_all(parts, 'pairs', split_axis=0, concat_axis=0)]
    all_to_all x1, waiting for transfers between devices: 62 us -> 71.6 us  [on_device(): lax.all_to_all(spectra[:, send_rows], 'pairs', split_axis=1, concat_axis=...]
  transfers between devices with their start and end apart: 2 -> 3, of which waited for: 2 -> 2; matrix products, arithmetic and copies ran while one was open for 0% -> 43% of each run, Pallas kernels for 0% -> 0%
where the time goes in v1:
time: 487 us; the launch traced here: 486 us
  other arithmetic  226 us (46%)
  waiting for transfers between devices  104 us (21%)
  matrix products  62 us (13%)
  local copies, waits for them, and re-layouts  54 us (11%)
  starting transfers between devices  21.4 us (4%)
  between operations  13.6 us (3%)
  loops' own time  5.63 us (1%)
    another operation x13, other arithmetic  163 us
    all_to_all x1, waiting for transfers between devices, on_device(): lax.all_to_all(spectra[:, send_rows], 'pairs', split_axis=1, concat_axis=...  71.6 us
    cos x8, other arithmetic, lag_block(): lag_table = jnp.concatenate([jnp.cos(angles), -jnp.sin(angles)], axis=1)  51.4 us
    dot_general x12, matrix products, add_block(): jnp.dot(segment, cos_table, preferred_element_type=jnp.float32)  38.1 us
    reduce_scatter x1, waiting for transfers between devices, on_device(): lax.psum_scatter(lag_rows(stacked, lax.axis_size('tm') * lag_share, block...  32.4 us
    dot_general x8, matrix products, lag_block(): lax.dot_general(lag_table, stacked, (((1,), (1,)), ((), ())), precision=l...  23.9 us
    gather x1, local copies, waits for them, and re-layouts, on_device(): slot_ids = station_slot[every_pair.reshape(blocks, 2 * pair_count)]  23 us
    gather x1, local copies, waits for them, and re-layouts, on_device(): spectra[:, send_rows]  13 us
  transfers between devices with their start and end apart: 3, of which 2 were waited for; matrix products, arithmetic and copies ran while one was open for 43% of the time, Pallas kernels for 0%

profile of v1, /device:TPU:2, one launch (start us, length us, event | category | flops | bytes accessed | tf_op | source)
XLA Modules:
  0.0 486.4 jit_solution(18329330085008356647)
XLA Ops:
  7.9 11.6 %all-to-all-start = ((s32[32,1,128]{2,1,0:T(1,128)}), s32[32,1,128]{2,1,0:T(1,128)S(1)}, u32[]{:S(2)}, u32[]{:S(2)}) async-start(s32[32,1,128]{2,1,0:T(1,128)} %reshape.191), calls=%async_computation | async-start | bytes 32768 | tf_op jit(solution)/shard_map/all_to_all | solution.py:100
  24.1 200.6 %while.29 = (s32[]{:T(128)}, f32[128,3072]{1,0:T(8,128)}, bf16[128,6144]{1,0:T(8,128)(2,1)}, s32[]{:T(128)}, s32[]{:T(128)}, /*index=5*/s32[]{:T(128)}, s32[]{:T(128)}) while((s32[]{:T(128)}, f32[128,3072]{1,0:T(8,128)}, bf16[128,6144]{1,0:T(8,128)(2,1)}, s32[]{:T(128)}, s32[]{:T(128)}, /*index=5*/s32[]{:T(128)}, s32[]{:T(128)}) %tuple.80), condition=%wide.region_2.3_spmd.clone, body=%wide.region_1.2_spmd.clone.sunk | while | flops 419170304 | bytes 9584781 | solution.py:48
  24.1 13.5 %cosine_convert_fusion.2 = (bf16[512,1536]{1,0:T(8,128)(2,1)S(1)}, bf16[512,1536]{1,0:T(8,128)(2,1)S(1)}) fusion(s32[1536]{0:T(1024)S(1)} %iota_add_fusion.7, s32[512]{0:T(512)S(1)} %iota_add_fusion.8), kind=kLoop, calls=%fused_computation.29.clone.1 | loop fusion | flops 9437184 | bytes 3153920 | tf_op jit(solution)/shard_map/convert
  40.3 13.5 %cosine_convert_fusion.2 = (bf16[512,1536]{1,0:T(8,128)(2,1)S(1)}, bf16[512,1536]{1,0:T(8,128)(2,1)S(1)}) fusion(s32[1536]{0:T(1024)S(1)} %iota_add_fusion.7, s32[512]{0:T(512)S(1)} %iota_add_fusion.8), kind=kLoop, calls=%fused_computation.29.clone.1 | loop fusion | flops 9437184 | bytes 3153920 | tf_op jit(solution)/shard_map/convert
  53.8 3.2 convolution_add_fusion.2
  57.0 13.5 %cosine_convert_fusion.2 = (bf16[512,1536]{1,0:T(8,128)(2,1)S(1)}, bf16[512,1536]{1,0:T(8,128)(2,1)S(1)}) fusion(s32[1536]{0:T(1024)S(1)} %iota_add_fusion.7, s32[512]{0:T(512)S(1)} %iota_add_fusion.8), kind=kLoop, calls=%fused_computation.29.clone.1 | loop fusion | flops 9437184 | bytes 3153920 | tf_op jit(solution)/shard_map/convert
  70.6 3.2 convolution_add_fusion.2
  73.8 13.5 %cosine_convert_fusion.2 = (bf16[512,1536]{1,0:T(8,128)(2,1)S(1)}, bf16[512,1536]{1,0:T(8,128)(2,1)S(1)}) fusion(s32[1536]{0:T(1024)S(1)} %iota_add_fusion.7, s32[512]{0:T(512)S(1)} %iota_add_fusion.8), kind=kLoop, calls=%fused_computation.29.clone.1 | loop fusion | flops 9437184 | bytes 3153920 | tf_op jit(solution)/shard_map/convert
  87.3 3.2 convolution_add_fusion.2
  90.6 13.5 %cosine_convert_fusion.2 = (bf16[512,1536]{1,0:T(8,128)(2,1)S(1)}, bf16[512,1536]{1,0:T(8,128)(2,1)S(1)}) fusion(s32[1536]{0:T(1024)S(1)} %iota_add_fusion.7, s32[512]{0:T(512)S(1)} %iota_add_fusion.8), kind=kLoop, calls=%fused_computation.29.clone.1 | loop fusion | flops 9437184 | bytes 3153920 | tf_op jit(solution)/shard_map/convert
  104.1 3.2 convolution_add_fusion.2
  107.3 13.5 %cosine_convert_fusion.2 = (bf16[512,1536]{1,0:T(8,128)(2,1)S(1)}, bf16[512,1536]{1,0:T(8,128)(2,1)S(1)}) fusion(s32[1536]{0:T(1024)S(1)} %iota_add_fusion.7, s32[512]{0:T(512)S(1)} %iota_add_fusion.8), kind=kLoop, calls=%fused_computation.29.clone.1 | loop fusion | flops 9437184 | bytes 3153920 | tf_op jit(solution)/shard_map/convert
  120.9 3.2 convolution_add_fusion.2
  124.1 13.5 %cosine_convert_fusion.2 = (bf16[512,1536]{1,0:T(8,128)(2,1)S(1)}, bf16[512,1536]{1,0:T(8,128)(2,1)S(1)}) fusion(s32[1536]{0:T(1024)S(1)} %iota_add_fusion.7, s32[512]{0:T(512)S(1)} %iota_add_fusion.8), kind=kLoop, calls=%fused_computation.29.clone.1 | loop fusion | flops 9437184 | bytes 3153920 | tf_op jit(solution)/shard_map/convert
  137.6 3.2 convolution_add_fusion.2
  140.9 13.5 %cosine_convert_fusion.2 = (bf16[512,1536]{1,0:T(8,128)(2,1)S(1)}, bf16[512,1536]{1,0:T(8,128)(2,1)S(1)}) fusion(s32[1536]{0:T(1024)S(1)} %iota_add_fusion.7, s32[512]{0:T(512)S(1)} %iota_add_fusion.8), kind=kLoop, calls=%fused_computation.29.clone.1 | loop fusion | flops 9437184 | bytes 3153920 | tf_op jit(solution)/shard_map/convert
  154.4 3.2 convolution_add_fusion.2
  157.6 13.5 %cosine_convert_fusion.2 = (bf16[512,1536]{1,0:T(8,128)(2,1)S(1)}, bf16[512,1536]{1,0:T(8,128)(2,1)S(1)}) fusion(s32[1536]{0:T(1024)S(1)} %iota_add_fusion.7, s32[512]{0:T(512)S(1)} %iota_add_fusion.8), kind=kLoop, calls=%fused_computation.29.clone.1 | loop fusion | flops 9437184 | bytes 3153920 | tf_op jit(solution)/shard_map/convert
  171.2 3.2 convolution_add_fusion.2
  174.4 13.5 %cosine_convert_fusion.2 = (bf16[512,1536]{1,0:T(8,128)(2,1)S(1)}, bf16[512,1536]{1,0:T(8,128)(2,1)S(1)}) fusion(s32[1536]{0:T(1024)S(1)} %iota_add_fusion.7, s32[512]{0:T(512)S(1)} %iota_add_fusion.8), kind=kLoop, calls=%fused_computation.29.clone.1 | loop fusion | flops 9437184 | bytes 3153920 | tf_op jit(solution)/shard_map/convert
  187.9 3.2 convolution_add_fusion.2
  191.2 13.5 %cosine_convert_fusion.2 = (bf16[512,1536]{1,0:T(8,128)(2,1)S(1)}, bf16[512,1536]{1,0:T(8,128)(2,1)S(1)}) fusion(s32[1536]{0:T(1024)S(1)} %iota_add_fusion.7, s32[512]{0:T(512)S(1)} %iota_add_fusion.8), kind=kLoop, calls=%fused_computation.29.clone.1 | loop fusion | flops 9437184 | bytes 3153920 | tf_op jit(solution)/shard_map/convert
  204.7 3.2 convolution_add_fusion.2
  207.9 13.5 %cosine_convert_fusion.2 = (bf16[512,1536]{1,0:T(8,128)(2,1)S(1)}, bf16[512,1536]{1,0:T(8,128)(2,1)S(1)}) fusion(s32[1536]{0:T(1024)S(1)} %iota_add_fusion.7, s32[512]{0:T(512)S(1)} %iota_add_fusion.8), kind=kLoop, calls=%fused_computation.29.clone.1 | loop fusion | flops 9437184 | bytes 3153920 | tf_op jit(solution)/shard_map/convert
  221.5 3.2 convolution_add_fusion.2
  229.9 23.0 %gather_fusion = s32[4096]{0:T(1024)S(1)} fusion(s32[2048]{0:T(1024)S(1)} %copy-done, s32[4096]{0:T(1024)S(1)} %bitcast_clamp_fusion), kind=kCustom, calls=%fused_computation | custom fusion | bytes 49152 | tf_op jit(solution)/shard_map/gather | solution.py:102
  253.1 3.3 fusion.31
  257.2 13.0 %gather_fusion.1 = bf16[256,2,3072]{2,1,0:T(2,128)(2,1)} fusion(bf16[2,64,3072]{2,0,1:T(2,128)(2,1)S(1)} %pad_maximum_fusion, s32[1024]{0:T(1024)S(1)} %pad_clamp_fusion.1), kind=kCustom, calls=%fused_computation.1 | custom fusion | bytes 6292480 | tf_op jit(solution)/shard_map/gather | solution.py:117
  270.3 9.8 %all-to-all-start.1 = ((bf16[2,32,8,3072]{3,0,2,1:T(2,128)(2,1)}), bf16[2,32,8,3072]{3,0,2,1:T(2,128)(2,1)S(1)}, u32[]{:S(2)}, u32[]{:S(2)}) async-start(bf16[2,32,8,3072]{3,0,2,1:T(2,128)(2,1)} %bitcast.71), calls=%async_computation.1 | async-start | bytes 6291456 | tf_op jit(solution)/shard_map/all_to_all | solution.py:116
  280.1 71.6 %all-to-all-done.1 = bf16[2,32,8,3072]{3,0,2,1:T(2,128)(2,1)S(1)} async-done(((bf16[2,32,8,3072]{3,0,2,1:T(2,128)(2,1)}), bf16[2,32,8,3072]{3,0,2,1:T(2,128)(2,1)S(1)}, u32[]{:S(2)}, u32[]{:S(2)}) %all-to-all-start.1) | async-done | bytes 3145760 | tf_op jit(solution)/shard_map/all_to_all | solution.py:116
  351.7 4.8 gather_fusion.2
  360.6 85.5 %while.28 = (s32[]{:T(128)}, f32[8,256,64]{1,2,0:T(8,128)S(1)}, s32[8]{0:T(128)S(1)}, f32[64,3072]{1,0:T(8,128)S(1)}, s32[]{:T(128)}, /*index=5*/s32[1]{0:T(128)}) while((s32[]{:T(128)}, f32[8,256,64]{1,2,0:T(8,128)S(1)}, s32[8]{0:T(128)S(1)}, f32[64,3072]{1,0:T(8,128)S(1)}, s32[]{:T(128)}, /*index=5*/s32[1]{0:T(128)}) %tuple.81), condition=%wide.region_9.10_spmd, body=%wide.region_8.9_spmd.sunk | while | flops 608700416 | bytes 7157861 | solution.py:88
  361.9 6.4 %fusion.51 = (f32[256,1536]{1,0:T(8,128)S(1)}, f32[256,1536]{1,0:T(8,128)S(1)}) fusion(s32[1536]{0:T(1024)S(1)} %iota_add_fusion.6, s32[256]{0:T(256)S(1)} %add_add_fusion.2), kind=kLoop, calls=%fused_computation.14.clone.1 | loop fusion | flops 3932160 | bytes 3152896 | tf_op jit(solution)/shard_map/while/body/eval_jaxpr/cos | solution.py:73
  368.3 3.0 fusion.52
  372.6 6.4 %fusion.51 = (f32[256,1536]{1,0:T(8,128)S(1)}, f32[256,1536]{1,0:T(8,128)S(1)}) fusion(s32[1536]{0:T(1024)S(1)} %iota_add_fusion.6, s32[256]{0:T(256)S(1)} %add_add_fusion.2), kind=kLoop, calls=%fused_computation.14.clone.1 | loop fusion | flops 3932160 | bytes 3152896 | tf_op jit(solution)/shard_map/while/body/eval_jaxpr/cos | solution.py:73
  379.0 3.0 fusion.52
  383.3 6.4 %fusion.51 = (f32[256,1536]{1,0:T(8,128)S(1)}, f32[256,1536]{1,0:T(8,128)S(1)}) fusion(s32[1536]{0:T(1024)S(1)} %iota_add_fusion.6, s32[256]{0:T(256)S(1)} %add_add_fusion.2), kind=kLoop, calls=%fused_computation.14.clone.1 | loop fusion | flops 3932160 | bytes 3152896 | tf_op jit(solution)/shard_map/while/body/eval_jaxpr/cos | solution.py:73
  389.7 3.0 fusion.52
  394.0 6.4 %fusion.51 = (f32[256,1536]{1,0:T(8,128)S(1)}, f32[256,1536]{1,0:T(8,128)S(1)}) fusion(s32[1536]{0:T(1024)S(1)} %iota_add_fusion.6, s32[256]{0:T(256)S(1)} %add_add_fusion.2), kind=kLoop, calls=%fused_computation.14.clone.1 | loop fusion | flops 3932160 | bytes 3152896 | tf_op jit(solution)/shard_map/while/body/eval_jaxpr/cos | solution.py:73
  400.4 3.0 fusion.52
  404.7 6.4 %fusion.51 = (f32[256,1536]{1,0:T(8,128)S(1)}, f32[256,1536]{1,0:T(8,128)S(1)}) fusion(s32[1536]{0:T(1024)S(1)} %iota_add_fusion.6, s32[256]{0:T(256)S(1)} %add_add_fusion.2), kind=kLoop, calls=%fused_computation.14.clone.1 | loop fusion | flops 3932160 | bytes 3152896 | tf_op jit(solution)/shard_map/while/body/eval_jaxpr/cos | solution.py:73
  411.1 3.0 fusion.52
  415.4 6.4 %fusion.51 = (f32[256,1536]{1,0:T(8,128)S(1)}, f32[256,1536]{1,0:T(8,128)S(1)}) fusion(s32[1536]{0:T(1024)S(1)} %iota_add_fusion.6, s32[256]{0:T(256)S(1)} %add_add_fusion.2), kind=kLoop, calls=%fused_computation.14.clone.1 | loop fusion | flops 3932160 | bytes 3152896 | tf_op jit(solution)/shard_map/while/body/eval_jaxpr/cos | solution.py:73
  421.8 3.0 fusion.52
  426.1 6.4 %fusion.51 = (f32[256,1536]{1,0:T(8,128)S(1)}, f32[256,1536]{1,0:T(8,128)S(1)}) fusion(s32[1536]{0:T(1024)S(1)} %iota_add_fusion.6, s32[256]{0:T(256)S(1)} %add_add_fusion.2), kind=kLoop, calls=%fused_computation.14.clone.1 | loop fusion | flops 3932160 | bytes 3152896 | tf_op jit(solution)/shard_map/while/body/eval_jaxpr/cos | solution.py:73
  432.5 3.0 fusion.52
  436.8 6.4 %fusion.51 = (f32[256,1536]{1,0:T(8,128)S(1)}, f32[256,1536]{1,0:T(8,128)S(1)}) fusion(s32[1536]{0:T(1024)S(1)} %iota_add_fusion.6, s32[256]{0:T(256)S(1)} %add_add_fusion.2), kind=kLoop, calls=%fused_computation.14.clone.1 | loop fusion | flops 3932160 | bytes 3152896 | tf_op jit(solution)/shard_map/while/body/eval_jaxpr/cos | solution.py:73
  447.1 32.4 %reduce-scatter.2.cloned.1.call-done = f32[256,64]{0,1:T(8,128)} async-done(((f32[2048,64]{0,1:T(8,128)}), f32[256,64]{0,1:T(8,128)}) %reduce-scatter.2.cloned.1.call-update) | async-done | bytes 65552 | tf_op jit(solution)/shard_map/reduce_scatter | solution.py:127
  (99 shorter events, 27.5 us)
Async XLA Ops:
  6.5 223.3 %copy-start = (s32[2048]{0:T(1024)S(1)}, s32[2048]{0:T(1024)}, u32[]{:S(2)}) copy-start(s32[2048]{0:T(1024)} %param.8) | copy-start | bytes 24580
  7.9 220.4 %all-to-all-start = ((s32[32,1,128]{2,1,0:T(1,128)}), s32[32,1,128]{2,1,0:T(1,128)S(1)}, u32[]{:S(2)}, u32[]{:S(2)}) async-start(s32[32,1,128]{2,1,0:T(1,128)} %reshape.191), calls=%async_computation | async-start | bytes 32768 | tf_op jit(solution)/shard_map/all_to_all | solution.py:100
  19.7 2.8 copy-start.1
  224.7 1.9 copy-start.2
  270.3 81.5 %all-to-all-start.1 = ((bf16[2,32,8,3072]{3,0,2,1:T(2,128)(2,1)}), bf16[2,32,8,3072]{3,0,2,1:T(2,128)(2,1)S(1)}, u32[]{:S(2)}, u32[]{:S(2)}) async-start(bf16[2,32,8,3072]{3,0,2,1:T(2,128)(2,1)} %bitcast.71), calls=%async_computation.1 | async-start | bytes 6291456 | tf_op jit(solution)/shard_map/all_to_all | solution.py:116
  280.1 199.5 %reduce-scatter.2.cloned.1.call-start = ((), (), s32[]{:S(2)}) async-start(), calls=%async_computation.3 | async-start | bytes 589824 | tf_op jit(solution)/shard_map/reduce_scatter | solution.py:127
  359.6 1.0 copy-start.3
Sparse Core Ops, SparseCore 0:
  447.2 32.2 reduce-scatter.1
